TPU v7x, 512 devices: a whole 4x8x8 slice. The times are simulated.
512 devices in a mesh: dp: 16 (over z_hi, y), expert: 32 (over x, z_lo, core).
Axes of the slice: x: 4, y: 8, z: 8 (z_hi: 2, z_lo: 4; z = z_hi * 4 + z_lo), core: 2. Of those that a mesh axis runs over, the one named last changes fastest.
Arguments:
- layer_input: bfloat16 [65536, 640], P(('dp', 'expert')), may hold values from -6 to 6
- output_grad: bfloat16 [65536, 640], P(('dp', 'expert')), may hold values from -6 to 6
- gate_weights: float32 [65536, 2], P(('dp', 'expert')), may hold values from 0.1 to 1
- expert_ids: int32 [65536, 2], P(('dp', 'expert')), may hold values from 0 to 31, as said below
- slot_positions: int32 [65536, 2], P(('dp', 'expert')), may hold values from 0 to 5, as said below
- keep_mask: int32 [65536, 2], P(('dp', 'expert')), may hold values from 0 to 1, as said below
- weight_in: bfloat16 [32, 640, 5120], P('expert', None, 'dp'), may hold values from -0.25 to 0.25
- weight_out: bfloat16 [32, 5120, 640], P('expert', 'dp'), may hold values from -0.078125 to 0.078125
Outputs:
- input_grad: bfloat16 [65536, 640], P(('dp', 'expert'))
- weight_in_grad: bfloat16 [32, 640, 5120], P('expert', None, 'dp')
- weight_out_grad: bfloat16 [32, 5120, 640], P('expert', 'dp')
Inputs may be any that keep to these rules, and one draw needn't show every extreme that they name: `expert_ids`: a token's two experts differ. `slot_positions`: within the tokens of one device, taken in order with a token's first choice before its second, the choices naming one expert take positions 0, 1, 2 and so on; a choice at position 6 or beyond is dropped and has slot 0; kept choices of one device and expert have distinct slots. `keep_mask`: 1 exactly where the choice's position is below 6.
All inputs are finite; a program needn't handle non-finite values.
Results may differ from a plain program's by a relative error of at most 0.015.
Values may be sent and summed in bfloat16 or wider, within the bound.
A program may use at most 64 MiB of HBM per device.

v0:
```python
import jax
import jax.numpy as jnp
from jax import lax
from jax.sharding import PartitionSpec as P

root_coef = 0.7978845608028654
cube_coef = 0.044715


def gelu_value(preact):
    inner_arg = root_coef * (preact + cube_coef * preact * preact * preact)
    return 0.5 * preact * (1.0 + jnp.tanh(inner_arg))


def gelu_slope(preact):
    inner_arg = root_coef * (preact + cube_coef * preact * preact * preact)
    tanh_value = jnp.tanh(inner_arg)
    return 0.5 * (1.0 + tanh_value) + 0.5 * preact * (1.0 - tanh_value * tanh_value) * root_coef * (
        1.0 + 3.0 * cube_coef * preact * preact
    )


def expert_grads(pieces, weight_in, weight_out, local_experts):
    piece_in, piece_cot = pieces
    groups, owners, merged_slots, feature_width = piece_in.shape
    slot_cap = merged_slots // local_experts
    rows_in = piece_in.reshape(groups, owners, local_experts, slot_cap, feature_width)
    rows_cot = piece_cot.reshape(groups, owners, local_experts, slot_cap, feature_width)
    preact = jnp.einsum("gjlcd,ldf->gjlcf", rows_in, weight_in, preferred_element_type=jnp.float32)
    hidden = gelu_value(preact).astype(jnp.bfloat16)
    backprop = jnp.einsum(
        "gjlcd,lfd->gjlcf", rows_cot, weight_out, preferred_element_type=jnp.float32
    )
    grad_pre = (gelu_slope(preact) * backprop).astype(jnp.bfloat16)
    total_in = jnp.einsum("gjlcd,gjlcf->ldf", rows_in, grad_pre, preferred_element_type=jnp.float32)
    total_out = jnp.einsum("gjlcf,gjlcd->lfd", hidden, rows_cot, preferred_element_type=jnp.float32)
    return (total_in, total_out, grad_pre)


def body(
    layer_input,
    output_grad,
    gate_weights,
    expert_ids,
    slot_positions,
    keep_mask,
    weight_in,
    weight_out,
):
    token_count, feature_width = layer_input.shape
    owner_count = lax.axis_size("expert")
    local_experts = weight_in.shape[0]
    expert_total = local_experts * owner_count
    slot_cap = 3 * token_count // (2 * expert_total)
    bucket_total = expert_total * slot_cap
    target = (expert_ids * slot_cap + slot_positions).reshape(-1)
    kept_rows = keep_mask.reshape(-1) > 0
    columns = lax.broadcasted_iota(jnp.int32, (2 * token_count, bucket_total), 1)
    selector = ((columns == target[:, None]) & kept_rows[:, None]).astype(jnp.bfloat16)
    repeated_input = jnp.repeat(layer_input, 2, axis=0)
    scaled = (
        gate_weights.reshape(-1, 1) * jnp.repeat(output_grad, 2, axis=0).astype(jnp.float32)
    ).astype(jnp.bfloat16)
    send_input = jnp.einsum(
        "rb,rd->bd", selector, repeated_input, preferred_element_type=jnp.float32
    ).astype(jnp.bfloat16)
    send_cotan = jnp.einsum(
        "rb,rd->bd", selector, scaled, preferred_element_type=jnp.float32
    ).astype(jnp.bfloat16)
    send_input = send_input.reshape(owner_count, local_experts * slot_cap, feature_width)
    send_cotan = send_cotan.reshape(owner_count, local_experts * slot_cap, feature_width)
    arrived_input, arrived_cotan = (
        lax.all_to_all(send_input, "expert", split_axis=0, concat_axis=0, tiled=True),
        lax.all_to_all(send_cotan, "expert", split_axis=0, concat_axis=0, tiled=True),
    )
    total_in, total_out, grad_all = expert_grads(
        (
            lax.all_gather(arrived_input[None], "dp", axis=0, tiled=True),
            lax.all_gather(arrived_cotan[None], "dp", axis=0, tiled=True),
        ),
        weight_in,
        weight_out,
        local_experts,
    )
    summed = lax.psum_scatter(
        jnp.einsum(
            "gjlcf,ldf->gjlcd", grad_all, weight_in, preferred_element_type=jnp.float32
        ).astype(jnp.bfloat16),
        "dp",
        scatter_dimension=0,
        tiled=True,
    )
    own_rows = summed.reshape(owner_count, local_experts * slot_cap, feature_width)
    back_rows = lax.all_to_all(own_rows, "expert", split_axis=0, concat_axis=0, tiled=True).reshape(
        bucket_total, feature_width
    )
    picked = jnp.einsum(
        "rb,bd->rd", selector, back_rows, preferred_element_type=jnp.float32
    ).reshape(token_count, 2, feature_width)
    input_grad = jnp.sum(picked, axis=1).astype(jnp.bfloat16)
    return (input_grad, total_in.astype(jnp.bfloat16), total_out.astype(jnp.bfloat16))


def solution(mesh):
    in_specs = (
        P(("dp", "expert"), None),
        P(("dp", "expert"), None),
        P(("dp", "expert"), None),
        P(("dp", "expert"), None),
        P(("dp", "expert"), None),
        P(("dp", "expert"), None),
        P("expert", None, "dp"),
        P("expert", "dp", None),
    )
    out_specs = (P(("dp", "expert"), None), P("expert", None, "dp"), P("expert", "dp", None))
    return jax.shard_map(body, mesh=mesh, in_specs=in_specs, out_specs=out_specs, check_vma=False)
```

profile of v0, /device:TPU:1, one launch (start us, length us, event | category | flops | bytes accessed | tf_op | source)
XLA Modules:
  0.0 569.6 jit_solution(13144930978062049705)
XLA Ops:
  7.2 0.7 broadcast_compare_fusion
  8.0 0.1 copy.26
  8.1 0.1 gt.16
  8.2 0.7 multiply_add_fusion.1
  8.9 0.1 copy.25
  9.1 0.1 eq.30
  9.2 1.1 broadcast_in_dim.13
  10.3 0.1 reshape.96
  10.4 0.4 convolution_convert_fusion.1
  10.8 0.1 reshape.97
  10.9 23.8 %all_to_all.15 = bf16[32,6,640]{2,1,0:T(8,128)(2,1)S(1)} all-to-all(bf16[32,6,640]{2,1,0:T(8,128)(2,1)S(1)} %reshape.97), channel_id=1, replica_groups=mesh['dp'=16,'expert'=32] {'expert'}, dimensions={0} | all-to-all | bytes 491520 | tf_op jit(solution)/shard_map/all_to_all | solution.py:73
  34.7 0.7 copy.27
  35.5 0.8 copy.29
  36.3 0.1 mul.81
  36.4 1.1 broadcast_in_dim.15
  37.5 0.5 convert_element_type.52
  38.0 0.4 convolution_convert_fusion
  38.5 16.0 %all_to_all.16 = bf16[32,6,640]{2,1,0:T(8,128)(2,1)S(1)} all-to-all(bf16[32,6,640]{2,1,0:T(8,128)(2,1)S(1)} %reshape.99), channel_id=1, replica_groups=mesh['dp'=16,'expert'=32] {'expert'}, dimensions={0} | all-to-all | bytes 491520 | tf_op jit(solution)/shard_map/all_to_all | solution.py:74
  54.5 0.7 copy.30
  55.3 105.7 %all-gather.5.cloned.1.call-done = bf16[512,6,640]{2,0,1:T(8,128)(2,1)} async-done(((bf16[32,6,640]{2,0,1:T(8,128)(2,1)}), bf16[512,6,640]{2,0,1:T(8,128)(2,1)}) %all-gather.5.cloned.1.call-update) | async-done | bytes 3932176 | tf_op jit(solution)/shard_map/all_gather | solution.py:78
  161.0 6.7 %fusion.9 = f32[16,32,6,320]{3,1,2,0:T(8,128)} fusion(bf16[16,32,6,640]{3,1,0,2:T(8,128)(2,1)} %bitcast.90, bf16[1,640,320]{1,2,0:T(8,128)(2,1)S(1)} %copy-done), kind=kOutput, calls=%fused_computation.13 | convolution fusion | flops 1258291200 | bytes 8273920 | tf_op jit(solution)/shard_map/gjlcd,ldf->gjlcf/dot_general | solution.py:29
  167.7 120.5 %all-gather.7.cloned.1.call-done = bf16[512,6,640]{2,0,1:T(8,128)(2,1)} async-done(((bf16[32,6,640]{2,0,1:T(8,128)(2,1)}), bf16[512,6,640]{2,0,1:T(8,128)(2,1)}) %all-gather.7.cloned.1.call-update) | async-done | bytes 3932176 | tf_op jit(solution)/shard_map/all_gather | solution.py:79
  288.2 8.1 %fusion.16 = bf16[16,32,6,320]{3,1,2,0:T(8,128)(2,1)S(1)} fusion(f32[16,32,6,320]{3,1,2,0:T(8,128)} %fusion.9, bf16[16,32,6,640]{3,1,0,2:T(8,128)(2,1)} %bitcast.92, bf16[1,320,640]{2,1,0:T(8,128)(2,1)S(1)} %copy-done.1), kind=kOutput, calls=%fused_computation.21 | convolution fusion | flops 1276968960 | bytes 10240000 | tf_op jit(solution)/shard_map/gjlcd,lfd->gjlcf/dot_general | solution.py:31
  296.3 3.9 convert_bitcast_fusion
  300.2 6.4 %fusion.31 = bf16[1,320,640]{2,1,0:T(8,128)(2,1)} fusion(bf16[16,32,6,640]{3,1,0,2:T(8,128)(2,1)} %bitcast.93, f32[16,32,6,320]{3,1,2,0:T(8,128)} %fusion.9), kind=kOutput, calls=%fused_computation.27 | convolution fusion | flops 1267343360 | bytes 8273920 | tf_op jit(solution)/shard_map/gjlcf,gjlcd->lfd/dot_general | solution.py:36
  306.6 232.1 %reduce-scatter.2.cloned.1.call-done = bf16[1,32,1,6,640]{4,1,3,0,2:T(8,128)(2,1)} async-done(((bf16[16,32,1,6,640]{4,1,3,0,2:T(8,128)(2,1)}), bf16[1,32,1,6,640]{4,1,3,0,2:T(8,128)(2,1)}) %reduce-scatter.2.cloned.1.call-update) | async-done | bytes 245776 | tf_op jit(solution)/shard_map/reduce_scatter | solution.py:85
  538.7 1.8 copy.32
  540.5 8.9 %all-to-all-start.2 = ((bf16[32,6,640]{2,1,0:T(8,128)(2,1)}), bf16[32,6,640]{2,1,0:T(8,128)(2,1)S(1)}, u32[]{:S(2)}, u32[]{:S(2)}) async-start(bf16[32,6,640]{2,1,0:T(8,128)(2,1)} %copy.32), calls=%async_computation.3 | async-start | bytes 655360 | tf_op jit(solution)/shard_map/all_to_all | solution.py:94
  549.3 4.6 fusion.34
  554.0 8.0 %all-to-all-done.2 = bf16[32,6,640]{2,1,0:T(8,128)(2,1)S(1)} async-done(((bf16[32,6,640]{2,1,0:T(8,128)(2,1)}), bf16[32,6,640]{2,1,0:T(8,128)(2,1)S(1)}, u32[]{:S(2)}, u32[]{:S(2)}) %all-to-all-start.2) | async-done | bytes 245792 | tf_op jit(solution)/shard_map/all_to_all | solution.py:94
  562.0 0.1 reshape.109
  562.1 1.0 convolution_reduce_fusion
  (11 shorter events, 0.3 us)
Async XLA Ops:
  7.2 153.8 %copy-start = (bf16[1,640,320]{1,2,0:T(8,128)(2,1)S(1)}, bf16[1,640,320]{1,2,0:T(8,128)(2,1)}, u32[]{:S(2)}) copy-start(bf16[1,640,320]{1,2,0:T(8,128)(2,1)} %param.14) | copy-start | bytes 1228804
  7.2 153.8 %all-gather.5.cloned.1.call-start = ((), (), s32[]{:S(2)}) async-start(), calls=%async_computation.5 | async-start | bytes 4177920 | tf_op jit(solution)/shard_map/all_gather | solution.py:78
  35.5 252.7 %all-gather.7.cloned.1.call-start = ((), (), s32[]{:S(2)}) async-start(), calls=%async_computation.6 | async-start | bytes 4177920 | tf_op jit(solution)/shard_map/all_gather | solution.py:79
  55.3 232.9 %copy-start.1 = (bf16[1,320,640]{2,1,0:T(8,128)(2,1)S(1)}, bf16[1,320,640]{2,1,0:T(8,128)(2,1)}, u32[]{:S(2)}) copy-start(bf16[1,320,640]{2,1,0:T(8,128)(2,1)} %param.15) | copy-start | bytes 1228804
  55.3 483.4 %reduce-scatter.2.cloned.1.call-start = ((), (), s32[]{:S(2)}) async-start(), calls=%async_computation.4 | async-start | bytes 4177920 | tf_op jit(solution)/shard_map/reduce_scatter | solution.py:85
  540.5 21.5 %all-to-all-start.2 = ((bf16[32,6,640]{2,1,0:T(8,128)(2,1)}), bf16[32,6,640]{2,1,0:T(8,128)(2,1)S(1)}, u32[]{:S(2)}, u32[]{:S(2)}) async-start(bf16[32,6,640]{2,1,0:T(8,128)(2,1)} %copy.32), calls=%async_computation.3 | async-start | bytes 655360 | tf_op jit(solution)/shard_map/all_to_all | solution.py:94
Sparse Core Ops, SparseCore 0:
  35.6 125.3 all-gather.4
  164.7 123.4 all-gather.6
  300.3 238.3 reduce-scatter.1
where the time goes:
time: 570 us
  waiting for transfers between devices  466 us (82%)
  blocking collectives  39.8 us (7%)
  matrix products  31.5 us (6%)
  between operations  13.8 us (2%)
  starting transfers between devices  8.99 us (2%)
  local copies, waits for them, and re-layouts  7.68 us (1%)
    reduce_scatter x1, waiting for transfers between devices, body(): lax.psum_scatter(jnp.einsum('gjlcf,ldf->gjlcd', grad_all, weight_in, pref...  232 us
    all_gather x1, waiting for transfers between devices, body(): lax.all_gather(arrived_cotan[None], 'dp', axis=0, tiled=True)  120 us
    all_gather x1, waiting for transfers between devices, body(): lax.all_gather(arrived_input[None], 'dp', axis=0, tiled=True)  106 us
    all_to_all x1, blocking collectives, body(): lax.all_to_all(send_input, 'expert', split_axis=0, concat_axis=0, tiled=T...  23.8 us
    all_to_all x1, blocking collectives, body(): lax.all_to_all(send_cotan, 'expert', split_axis=0, concat_axis=0, tiled=T...  16 us
  transfers between devices with their start and end apart: 4, of which 4 were waited for; matrix products, arithmetic and copies ran while one was open for 4% of the time, Pallas kernels for 0%

commit v1 on v0

v1 whole, which is shorter than its diff:
```python
import jax
import jax.numpy as jnp
from jax import lax
from jax.experimental import pallas as pl
from jax.experimental.pallas import tpu as pltpu
from jax.sharding import PartitionSpec as P

MESH = pl.DeviceIdType.MESH
ROOT_COEF = 0.7978845608028654
CUBE_COEF = 0.044715
N_EXP = 32
N_Y = 8
CAP = 6
ROWS = N_EXP * CAP
HALF = ROWS // 2
BF16 = jnp.bfloat16
F32 = jnp.float32


def dot(a, b, dims):
    return lax.dot_general(a, b, (dims, ((), ())), preferred_element_type=F32)


NN = ((1,), (0,))
NT = ((1,), (1,))
TN = ((0,), (0,))


def iota(shape, dim):
    return lax.broadcasted_iota(jnp.int32, shape, dim)


def column(row):
    n = row.shape[1]
    eye = iota((n, n), 0) == iota((n, n), 1)
    return jnp.sum(jnp.where(eye, jnp.broadcast_to(row, (n, n)), 0.0), axis=1, keepdims=True)


def kernel(
    x_ref, g_ref, gate_ref, eid_ref, slot_ref, keep_ref, win_ref, wout_ref,
    out_ref, owin_ref, owout_ref,
    send, recv, rows, part, wp, dw, dw_out, dw_in, gp, rs_out, rs_in, back_out, back_in,
    a2a_s, a2a_r, ag_s, ag_r, w_s, w_r, dw_s, dw_r, rs_s, rs_r, back_s, back_r,
):
    d = lax.axis_index("dp")
    e = lax.axis_index("expert")
    y = lax.rem(d, N_Y)
    base = d - y
    right = (base + lax.rem(y + 1, N_Y), e)
    left = (base + lax.rem(y + N_Y - 1, N_Y), e)
    mate = (lax.rem(d + N_Y, 2 * N_Y), e)
    side = (right, left)

    def remote(src, dst, ssem, rsem, device):
        return pltpu.make_async_remote_copy(
            src_ref=src, dst_ref=dst, send_sem=ssem, recv_sem=rsem,
            device_id=device, device_id_type=MESH,
        )

    barrier = pltpu.get_barrier_semaphore()

    def greet(k, c):
        pl.semaphore_signal(barrier, 1, device_id=(d, lax.rem(e + k, N_EXP)), device_id_type=MESH)
        return c

    lax.fori_loop(1, N_EXP, greet, 0)
    for device in (right, left, mate):
        pl.semaphore_signal(barrier, 1, device_id=device, device_id_type=MESH)

    tokens = x_ref.shape[0]
    eid = eid_ref[...].astype(F32)
    slot = slot_ref[...].astype(F32)
    kept = keep_ref[...] > 0
    target = jnp.where(kept, eid * 16.0 + slot, -100.0)
    blk = N_EXP * 16
    row_id = iota((blk, tokens), 0).astype(F32)
    hot_in = jnp.zeros((blk, tokens), F32)
    hots = []
    scaled = []
    grad = g_ref[...].astype(F32)
    for k in range(2):
        t = jnp.broadcast_to(target[k : k + 1], (blk, tokens))
        hot_in = hot_in + jnp.where(row_id == t, 1.0, 0.0)
        hots.append(jnp.where(row_id == t + 8.0, 1.0, 0.0).astype(BF16))
        scaled.append((column(gate_ref[k : k + 1]) * grad).astype(BF16))
    hot = jnp.concatenate([hot_in.astype(BF16)] + hots, axis=1)
    source = jnp.concatenate([x_ref[...]] + scaled, axis=0)
    send[...] = dot(hot, source, NN).astype(BF16).reshape(send.shape)
    recv[pl.ds(e, 1)] = send[pl.ds(e, 1)]
    dw[...] = jnp.zeros_like(dw)

    pl.semaphore_wait(barrier, N_EXP - 1 + 3)

    def a2a(k):
        t = lax.rem(e + k, N_EXP)
        return remote(send.at[t], recv.at[e], a2a_s.at[t], a2a_r.at[e], (d, t))

    def a2a_from(k):
        t = lax.rem(e + N_EXP - k, N_EXP)
        return remote(send.at[t], recv.at[t], a2a_s.at[t], a2a_r.at[t], (d, t))

    def a2a_start(k, c):
        a2a(k).start()
        return c

    def a2a_wait_recv(k, c):
        a2a_from(k).wait_recv()
        return c

    def a2a_wait_send(k, c):
        a2a(k).wait_send()
        return c

    lax.fori_loop(1, N_EXP, a2a_start, 0)
    weights = [
        remote(win_ref, wp.at[0], w_s.at[0], w_r.at[0], mate),
        remote(wout_ref, wp.at[1], w_s.at[1], w_r.at[1], mate),
    ]
    for copy in weights:
        copy.start()
    lax.fori_loop(1, N_EXP, a2a_wait_recv, 0)

    q = iota((ROWS, blk), 1)
    lane = jnp.bitwise_and(q, 7)
    want = jnp.where(lane < CAP, lax.shift_right_logical(q, 4) * CAP + lane, -1)
    which = jnp.bitwise_and(lax.shift_right_logical(q, 3), 1)
    at_row = iota((ROWS, blk), 0) == want
    arrived = recv[...].reshape(blk, -1)
    for s in range(2):
        close = jnp.where(at_row & (which == s), 1.0, 0.0).astype(BF16)
        rows[s, 0] = dot(close, arrived, NN).astype(BF16)

    def place(way, n):
        return 2 * n + way

    def gather(way, i, src_slot, dst_slot):
        s = lax.rem(i + way, 2)
        return remote(
            rows.at[s, src_slot], rows.at[s, dst_slot], ag_s.at[way, i], ag_r.at[way, i], side[way]
        )

    for i in range(2):
        for way in range(2):
            gather(way, i, 0, place(way, 1)).start()

    def core(b, half, wi, wo, gp_at):
        ri = rows[0, pl.ds(2 * b, 2)].reshape(2 * ROWS, -1)
        rc = rows[1, pl.ds(2 * b, 2)].reshape(2 * ROWS, -1)
        pre = dot(wi[...], ri, NT)
        bp = dot(wo[...], rc, NT)
        sq = pre * pre
        h = jnp.tanh(ROOT_COEF * (pre + CUBE_COEF * sq * pre))
        up = 0.5 * (1.0 + h)
        slope = up + 0.5 * pre * (1.0 - h * h) * ROOT_COEF * (1.0 + 3.0 * CUBE_COEF * sq)
        g = (slope * bp).astype(BF16)
        gp_at[...] = g
        dw[half, 0] += dot(g, ri, NN)
        dw[half, 1] += dot((pre * up).astype(BF16), rc, NN)

    def project(b, wi, gp_at, first):
        p = dot(gp_at[...], wi[...], TN).reshape(2, ROWS, -1)
        if first:
            part[pl.ds(2 * b, 2)] = p
        else:
            part[pl.ds(2 * b, 2)] += p

    def own_step(n, c):
        for j in range(2):
            i = 2 * (n - 1) + j
            for way in range(2):
                gather(way, i, 0, place(way, n)).wait_recv()

            def forward():
                for way in range(2):
                    dst = jnp.where(n == 3, 1, place(way, n + 1))
                    gather(way, i + 2, place(way, n), dst).start()

            if j == 0:
                forward()
            else:
                pl.when(n < 3)(forward)
        core(n, 0, win_ref, wout_ref, gp.at[0])
        project(n, win_ref, gp.at[0], True)
        return c

    lax.fori_loop(1, 4, own_step, 0)

    for copy in weights:
        copy.wait_recv()

    def mate_step(n, c):
        core(n, 1, wp.at[0], wp.at[1], gp.at[1])
        project(n, wp.at[0], gp.at[1], False)
        return c

    lax.fori_loop(1, 4, mate_step, 0)

    for way in range(2):
        gather(way, 6, place(way, 3), 1).wait_recv()
    core(0, 1, wp.at[0], wp.at[1], gp.at[1])
    dw_out[...] = dw[1].astype(BF16)
    deltas = [remote(dw_out.at[i], dw_in.at[i], dw_s.at[i], dw_r.at[i], mate) for i in range(2)]
    for copy in deltas:
        copy.start()
    core(0, 0, win_ref, wout_ref, gp.at[0])
    project(0, win_ref, gp.at[0], True)
    project(0, wp.at[0], gp.at[1], False)

    def ring(way, i):
        return remote(
            rs_out.at[way, i], rs_in.at[way, i], rs_s.at[way, i], rs_r.at[way, i], side[way]
        )

    def span(way, i):
        h = (i + way) % 2
        return pl.ds(h * HALF, HALF)

    for i in range(7):
        far = 4 - (i + 1) // 2
        for way in range(2):
            at = 1 if far == 4 else 2 * far + 1 - way
            value = part[at, span(way, i)]
            if i >= 2:
                ring(way, i - 2).wait_recv()
                value = value + rs_in[way, i - 2].astype(F32)
            rs_out[way, i] = value.astype(BF16)
            ring(way, i).start()

    spread_q = iota((N_EXP * 8, ROWS), 0)
    spread_lane = jnp.bitwise_and(spread_q, 7)
    spread_want = jnp.where(
        spread_lane < CAP, lax.shift_right_logical(spread_q, 3) * CAP + spread_lane, -1
    )
    spread = jnp.where(iota((N_EXP * 8, ROWS), 1) == spread_want, 1.0, 0.0).astype(BF16)
    pick = jnp.zeros((tokens, N_EXP * 8), F32)
    column_id = iota((tokens, N_EXP * 8), 1).astype(F32)
    for k in range(2):
        t = jnp.where(kept[k : k + 1], eid[k : k + 1] * 8.0 + slot[k : k + 1], -100.0)
        pick = pick + jnp.where(column_id == column(t), 1.0, 0.0)
    pick = pick.astype(BF16)

    for i in (5, 6):
        for way in range(2):
            ring(way, i).wait_recv()
    sums = []
    for h in range(2):
        value = part[0, pl.ds(h * HALF, HALF)]
        for way in range(2):
            i = 6 if (6 + way) % 2 == h else 5
            value = value + rs_in[way, i].astype(F32)
        sums.append(value.astype(BF16))
    total = jnp.concatenate(sums, axis=0)
    back_out[...] = dot(spread, total, NN).reshape(back_out.shape).astype(BF16)
    back_in[pl.ds(e, 1)] = back_out[pl.ds(e, 1)]

    def back(k):
        t = lax.rem(e + k, N_EXP)
        return remote(back_out.at[t], back_in.at[e], back_s.at[t], back_r.at[e], (d, t))

    def back_from(k):
        t = lax.rem(e + N_EXP - k, N_EXP)
        return remote(back_out.at[t], back_in.at[t], back_s.at[t], back_r.at[t], (d, t))

    def back_start(k, c):
        back(k).start()
        return c

    def back_wait_recv(k, c):
        back_from(k).wait_recv()
        return c

    def back_wait_send(k, c):
        back(k).wait_send()
        return c

    lax.fori_loop(1, N_EXP, back_start, 0)
    lax.fori_loop(1, N_EXP, a2a_wait_send, 0)
    for copy in weights:
        copy.wait_send()

    def gather_wait_send(i, c):
        for way in range(2):
            gather(way, i, 0, 1).wait_send()
        return c

    lax.fori_loop(0, 7, gather_wait_send, 0)
    for i in range(7):
        for way in range(2):
            ring(way, i).wait_send()
    lax.fori_loop(1, N_EXP, back_wait_recv, 0)
    returned = back_in[...].astype(F32).reshape(N_EXP * 8, -1).astype(BF16)
    out_ref[...] = dot(pick, returned, NN).astype(BF16)
    lax.fori_loop(1, N_EXP, back_wait_send, 0)

    for copy in deltas:
        copy.wait_recv()
    owin_ref[...] = (dw[0, 0] + dw_in[0].astype(F32)).astype(BF16)
    owout_ref[...] = (dw[0, 1] + dw_in[1].astype(F32)).astype(BF16)
    for copy in deltas:
        copy.wait_send()


def body(x, g, gate, eid, slot, keep, weight_in, weight_out):
    tokens, width = x.shape
    hidden = weight_in.shape[2]
    dma = pltpu.SemaphoreType.DMA
    vmem = pl.BlockSpec(memory_space=pltpu.VMEM)
    out, dwin, dwout = pl.pallas_call(
        kernel,
        out_shape=(
            jax.ShapeDtypeStruct((tokens, width), BF16),
            jax.ShapeDtypeStruct((hidden, width), BF16),
            jax.ShapeDtypeStruct((hidden, width), BF16),
        ),
        in_specs=[vmem] * 8,
        out_specs=(vmem, vmem, vmem),
        scratch_shapes=[
            pltpu.VMEM((N_EXP, 16, width), BF16),
            pltpu.VMEM((N_EXP, 16, width), BF16),
            pltpu.VMEM((2, N_Y, ROWS, width), BF16),
            pltpu.VMEM((N_Y, ROWS, width), F32),
            pltpu.VMEM((2, hidden, width), BF16),
            pltpu.VMEM((2, 2, hidden, width), F32),
            pltpu.VMEM((2, hidden, width), BF16),
            pltpu.VMEM((2, hidden, width), BF16),
            pltpu.VMEM((2, hidden, 2 * ROWS), BF16),
            pltpu.VMEM((2, 7, HALF, width), BF16),
            pltpu.VMEM((2, 7, HALF, width), BF16),
            pltpu.VMEM((N_EXP, 8, width), BF16),
            pltpu.VMEM((N_EXP, 8, width), BF16),
            dma((N_EXP,)), dma((N_EXP,)),
            dma((2, 7)), dma((2, 7)),
            dma((2,)), dma((2,)),
            dma((2,)), dma((2,)),
            dma((2, 7)), dma((2, 7)),
            dma((N_EXP,)), dma((N_EXP,)),
        ],
        compiler_params=pltpu.CompilerParams(
            collective_id=0, has_side_effects=True, vmem_limit_bytes=56 * 1024 * 1024
        ),
        name="moe_backward",
    )(
        x, g, gate.T, eid.T, slot.T, keep.T,
        jnp.swapaxes(weight_in[0], 0, 1), weight_out[0],
    )
    return out, jnp.swapaxes(dwin, 0, 1)[None], dwout[None]


def solution(mesh):
    split = P(("dp", "expert"), None)
    w_in, w_out = P("expert", None, "dp"), P("expert", "dp", None)
    return jax.shard_map(
        body, mesh=mesh, in_specs=(split,) * 6 + (w_in, w_out),
        out_specs=(split, w_in, w_out), check_vma=False,
    )
```

time: 570 us -> 161 us (0.28)
  waiting for transfers between devices: 466 us -> 0 us
  Pallas kernels: 0 us -> 156 us
  blocking collectives: 39.8 us -> 0 us
  matrix products: 31.5 us -> 0 us
  between operations: 13.8 us -> 0.64 us
  starting transfers between devices: 8.99 us -> 0 us
    reduce_scatter x1 -> x0, waiting for transfers between devices: 232 us -> none  [body(): lax.psum_scatter(jnp.einsum('gjlcf,ldf->gjlcd', grad_all, weight_in, pref...]
    all_gather x2 -> x0, waiting for transfers between devices: 226 us -> none  [the longest x1 120 us: body(): lax.all_gather(arrived_cotan[None], 'dp', axis=0, tiled=True)]
    pallas_call x0 -> x1, Pallas kernels: none -> 156 us  [body(): pl.pallas_call(kernel, out_shape=(jax.ShapeDtypeStruct((tokens, width), B...]
    all_to_all x2 -> x0, blocking collectives: 39.8 us -> none  [the longest x1 23.8 us: body(): lax.all_to_all(send_input, 'expert', split_axis=0, concat_axis=0, tiled=T...]
    dot_general x8 -> x0, matrix products: 31.5 us -> none  [the longest x1 8.15 us: expert_grads(): jnp.einsum('gjlcd,lfd->gjlcf', rows_cot, weight_out, preferred_element_ty...]
    all_to_all x1 -> x0, starting transfers between devices: 8.86 us -> none  [body(): lax.all_to_all(own_rows, 'expert', split_axis=0, concat_axis=0, tiled=True)]
    all_to_all x1 -> x0, waiting for transfers between devices: 7.99 us -> none  [body(): lax.all_to_all(own_rows, 'expert', split_axis=0, concat_axis=0, tiled=True)]
  transfers between devices with their start and end apart: 4 -> 0, of which waited for: 4 -> 0; matrix products, arithmetic and copies ran while one was open for 4% -> 0% of each run, Pallas kernels for 0% -> 0%
where the time goes in v1:
time: 161 us
  Pallas kernels  156 us (97%)
  local copies, waits for them, and re-layouts  4.19 us (3%)
    pallas_call x1, Pallas kernels, body(): pl.pallas_call(kernel, out_shape=(jax.ShapeDtypeStruct((tokens, width), B...  156 us
    unnamed x5, local copies, waits for them, and re-layouts  4.19 us

profile of v1, /device:TPU:1, one launch (start us, length us, event | category | flops | bytes accessed | tf_op | source)
XLA Modules:
  0.0 160.9 jit_solution(9294670619008939134)
XLA Ops:
  0.6 156.1 %moe_backward.1 = (bf16[128,640]{1,0:T(8,128)(2,1)}, bf16[320,640]{1,0:T(8,128)(2,1)}, bf16[320,640]{1,0:T(8,128)(2,1)}) custom-call(bf16[128,640]{1,0:T(8,128)(2,1)} %x_ref.1, bf16[128,640]{1,0:T(8,128)(2,1)} %g_ref.1, f32[2,128]{1,0:T(2,128)} %bitcast.16, s32[2,128]{1,0:T(2,128)} %bitcast.17, s32[2,128]{1,0:T(2,128)} %bitcast.18, s32[2,128]{1,0:T(2,128)} %bitcast.19, ...), custom_call_target="tpu_custom_call" | custom-call | tf_op jit(solution)/shard_map/moe_backward/pallas_call | solution.py:308
  156.7 1.6 copy.14
  158.3 0.0 copy-start
  158.3 1.8 %copy.15 = bf16[1,640,320]{1,2,0:T(8,128)(2,1)} copy(bf16[1,640,320]{1,2,0:T(8,128)(2,1)} %bitcast.15) | data formatting | bytes 819200
  160.2 0.0 copy-done
  160.2 0.8 copy.16
Async XLA Ops:
  158.3 1.8 %copy-start = (bf16[320,640]{1,0:T(8,128)(2,1)S(1)}, bf16[320,640]{1,0:T(8,128)(2,1)}, u32[]{:S(2)}) copy-start(bf16[320,640]{1,0:T(8,128)(2,1)} %get-tuple-element.8) | copy-start | bytes 1228804

commit v2 on v1

--- a/solution.py
+++ b/solution.py
@@ -68,80 +68,71 @@
         pl.semaphore_signal(barrier, 1, device_id=device, device_id_type=MESH)
 
     tokens = x_ref.shape[0]
+    blk = N_EXP * 8
     eid = eid_ref[...].astype(F32)
     slot = slot_ref[...].astype(F32)
-    kept = keep_ref[...] > 0
-    target = jnp.where(kept, eid * 16.0 + slot, -100.0)
-    blk = N_EXP * 16
+    target = jnp.where(keep_ref[...] > 0, eid * 8.0 + slot, -100.0)
     row_id = iota((blk, tokens), 0).astype(F32)
-    hot_in = jnp.zeros((blk, tokens), F32)
-    hots = []
-    scaled = []
+    hots = [
+        jnp.where(row_id == jnp.broadcast_to(target[k : k + 1], (blk, tokens)), 1.0, 0.0)
+        for k in range(2)
+    ]
+    send[0] = dot((hots[0] + hots[1]).astype(BF16), x_ref[...], NN).astype(BF16).reshape(send.shape[1:])
     grad = g_ref[...].astype(F32)
-    for k in range(2):
-        t = jnp.broadcast_to(target[k : k + 1], (blk, tokens))
-        hot_in = hot_in + jnp.where(row_id == t, 1.0, 0.0)
-        hots.append(jnp.where(row_id == t + 8.0, 1.0, 0.0).astype(BF16))
-        scaled.append((column(gate_ref[k : k + 1]) * grad).astype(BF16))
-    hot = jnp.concatenate([hot_in.astype(BF16)] + hots, axis=1)
-    source = jnp.concatenate([x_ref[...]] + scaled, axis=0)
-    send[...] = dot(hot, source, NN).astype(BF16).reshape(send.shape)
-    recv[pl.ds(e, 1)] = send[pl.ds(e, 1)]
+    scaled = [(column(gate_ref[k : k + 1]) * grad).astype(BF16) for k in range(2)]
+    send[1] = dot(
+        jnp.concatenate(hots, axis=1).astype(BF16), jnp.concatenate(scaled, axis=0), NN
+    ).astype(BF16).reshape(send.shape[1:])
+    for s in range(2):
+        recv[s, pl.ds(e, 1)] = send[s, pl.ds(e, 1)]
     dw[...] = jnp.zeros_like(dw)
 
     pl.semaphore_wait(barrier, N_EXP - 1 + 3)
 
-    def a2a(k):
+    def a2a(s, k):
         t = lax.rem(e + k, N_EXP)
-        return remote(send.at[t], recv.at[e], a2a_s.at[t], a2a_r.at[e], (d, t))
-
-    def a2a_from(k):
+        return remote(send.at[s, t], recv.at[s, e], a2a_s.at[s, t], a2a_r.at[s, e], (d, t))
+
+    def a2a_from(s, k):
         t = lax.rem(e + N_EXP - k, N_EXP)
-        return remote(send.at[t], recv.at[t], a2a_s.at[t], a2a_r.at[t], (d, t))
-
-    def a2a_start(k, c):
-        a2a(k).start()
-        return c
-
-    def a2a_wait_recv(k, c):
-        a2a_from(k).wait_recv()
-        return c
-
-    def a2a_wait_send(k, c):
-        a2a(k).wait_send()
-        return c
-
-    lax.fori_loop(1, N_EXP, a2a_start, 0)
+        return remote(send.at[s, t], recv.at[s, t], a2a_s.at[s, t], a2a_r.at[s, t], (d, t))
+
+    def each_peer(act):
+        def step(k, c):
+            act(k)
+            return c
+
+        lax.fori_loop(1, N_EXP, step, 0)
+
+    for s in range(2):
+        each_peer(lambda k: a2a(s, k).start())
+
+    q = iota((ROWS, blk), 1)
+    lane = jnp.bitwise_and(q, 7)
+    want = jnp.where(lane < CAP, lax.shift_right_logical(q, 3) * CAP + lane, -1)
+    close = jnp.where(iota((ROWS, blk), 0) == want, 1.0, 0.0).astype(BF16)
+
+    def gather(way, i):
+        s, n = i % 2, i // 2
+        sems = ag_s.at[way, i], ag_r.at[way, i], side[way]
+        src = 0 if n == 0 else 2 * n + way
+        if n == 3:
+            cut = pl.ds(way * HALF, HALF)
+            return remote(rows.at[s, src, cut], rows.at[s, 1, cut], *sems)
+        return remote(rows.at[s, src], rows.at[s, 2 * n + 2 + way], *sems)
+
     weights = [
         remote(win_ref, wp.at[0], w_s.at[0], w_r.at[0], mate),
         remote(wout_ref, wp.at[1], w_s.at[1], w_r.at[1], mate),
     ]
+    for s in range(2):
+        each_peer(lambda k: a2a_from(s, k).wait_recv())
+        arrived = recv[s].astype(F32).reshape(blk, -1).astype(BF16)
+        rows[s, 0] = dot(close, arrived, NN).astype(BF16)
+        for way in range(2):
+            gather(way, s).start()
     for copy in weights:
         copy.start()
-    lax.fori_loop(1, N_EXP, a2a_wait_recv, 0)
-
-    q = iota((ROWS, blk), 1)
-    lane = jnp.bitwise_and(q, 7)
-    want = jnp.where(lane < CAP, lax.shift_right_logical(q, 4) * CAP + lane, -1)
-    which = jnp.bitwise_and(lax.shift_right_logical(q, 3), 1)
-    at_row = iota((ROWS, blk), 0) == want
-    arrived = recv[...].reshape(blk, -1)
-    for s in range(2):
-        close = jnp.where(at_row & (which == s), 1.0, 0.0).astype(BF16)
-        rows[s, 0] = dot(close, arrived, NN).astype(BF16)
-
-    def place(way, n):
-        return 2 * n + way
-
-    def gather(way, i, src_slot, dst_slot):
-        s = lax.rem(i + way, 2)
-        return remote(
-            rows.at[s, src_slot], rows.at[s, dst_slot], ag_s.at[way, i], ag_r.at[way, i], side[way]
-        )
-
-    for i in range(2):
-        for way in range(2):
-            gather(way, i, 0, place(way, 1)).start()
 
     def core(b, half, wi, wo, gp_at):
         ri = rows[0, pl.ds(2 * b, 2)].reshape(2 * ROWS, -1)
@@ -164,26 +155,13 @@
         else:
             part[pl.ds(2 * b, 2)] += p
 
-    def own_step(n, c):
-        for j in range(2):
-            i = 2 * (n - 1) + j
+    for n in range(1, 4):
+        for i in (2 * n - 2, 2 * n - 1):
             for way in range(2):
-                gather(way, i, 0, place(way, n)).wait_recv()
-
-            def forward():
-                for way in range(2):
-                    dst = jnp.where(n == 3, 1, place(way, n + 1))
-                    gather(way, i + 2, place(way, n), dst).start()
-
-            if j == 0:
-                forward()
-            else:
-                pl.when(n < 3)(forward)
+                gather(way, i).wait_recv()
+                gather(way, i + 2).start()
         core(n, 0, win_ref, wout_ref, gp.at[0])
         project(n, win_ref, gp.at[0], True)
-        return c
-
-    lax.fori_loop(1, 4, own_step, 0)
 
     for copy in weights:
         copy.wait_recv()
@@ -195,8 +173,9 @@
 
     lax.fori_loop(1, 4, mate_step, 0)
 
-    for way in range(2):
-        gather(way, 6, place(way, 3), 1).wait_recv()
+    for i in (6, 7):
+        for way in range(2):
+            gather(way, i).wait_recv()
     core(0, 1, wp.at[0], wp.at[1], gp.at[1])
     dw_out[...] = dw[1].astype(BF16)
     deltas = [remote(dw_out.at[i], dw_in.at[i], dw_s.at[i], dw_r.at[i], mate) for i in range(2)]
@@ -226,17 +205,16 @@
             rs_out[way, i] = value.astype(BF16)
             ring(way, i).start()
 
-    spread_q = iota((N_EXP * 8, ROWS), 0)
+    spread_q = iota((blk, ROWS), 0)
     spread_lane = jnp.bitwise_and(spread_q, 7)
     spread_want = jnp.where(
         spread_lane < CAP, lax.shift_right_logical(spread_q, 3) * CAP + spread_lane, -1
     )
-    spread = jnp.where(iota((N_EXP * 8, ROWS), 1) == spread_want, 1.0, 0.0).astype(BF16)
-    pick = jnp.zeros((tokens, N_EXP * 8), F32)
-    column_id = iota((tokens, N_EXP * 8), 1).astype(F32)
+    spread = jnp.where(iota((blk, ROWS), 1) == spread_want, 1.0, 0.0).astype(BF16)
+    column_id = iota((tokens, blk), 1).astype(F32)
+    pick = jnp.zeros((tokens, blk), F32)
     for k in range(2):
-        t = jnp.where(kept[k : k + 1], eid[k : k + 1] * 8.0 + slot[k : k + 1], -100.0)
-        pick = pick + jnp.where(column_id == column(t), 1.0, 0.0)
+        pick = pick + jnp.where(column_id == column(target[k : k + 1]), 1.0, 0.0)
     pick = pick.astype(BF16)
 
     for i in (5, 6):
@@ -261,41 +239,24 @@
         t = lax.rem(e + N_EXP - k, N_EXP)
         return remote(back_out.at[t], back_in.at[t], back_s.at[t], back_r.at[t], (d, t))
 
-    def back_start(k, c):
-        back(k).start()
-        return c
-
-    def back_wait_recv(k, c):
-        back_from(k).wait_recv()
-        return c
-
-    def back_wait_send(k, c):
-        back(k).wait_send()
-        return c
-
-    lax.fori_loop(1, N_EXP, back_start, 0)
-    lax.fori_loop(1, N_EXP, a2a_wait_send, 0)
+    each_peer(lambda k: back(k).start())
+    for s in range(2):
+        each_peer(lambda k: a2a(s, k).wait_send())
     for copy in weights:
         copy.wait_send()
-
-    def gather_wait_send(i, c):
-        for way in range(2):
-            gather(way, i, 0, 1).wait_send()
-        return c
-
-    lax.fori_loop(0, 7, gather_wait_send, 0)
-    for i in range(7):
-        for way in range(2):
+    for way in range(2):
+        for i in range(8):
+            gather(way, i).wait_send()
+        for i in range(7):
             ring(way, i).wait_send()
-    lax.fori_loop(1, N_EXP, back_wait_recv, 0)
-    returned = back_in[...].astype(F32).reshape(N_EXP * 8, -1).astype(BF16)
+    each_peer(lambda k: back_from(k).wait_recv())
+    returned = back_in[...].astype(F32).reshape(blk, -1).astype(BF16)
     out_ref[...] = dot(pick, returned, NN).astype(BF16)
-    lax.fori_loop(1, N_EXP, back_wait_send, 0)
-
-    for copy in deltas:
-        copy.wait_recv()
-    owin_ref[...] = (dw[0, 0] + dw_in[0].astype(F32)).astype(BF16)
-    owout_ref[...] = (dw[0, 1] + dw_in[1].astype(F32)).astype(BF16)
+    each_peer(lambda k: back(k).wait_send())
+
+    for i, ref in ((0, owin_ref), (1, owout_ref)):
+        deltas[i].wait_recv()
+        ref[...] = (dw[0, i] + dw_in[i].astype(F32)).astype(BF16)
     for copy in deltas:
         copy.wait_send()
 
@@ -315,8 +276,8 @@
         in_specs=[vmem] * 8,
         out_specs=(vmem, vmem, vmem),
         scratch_shapes=[
-            pltpu.VMEM((N_EXP, 16, width), BF16),
-            pltpu.VMEM((N_EXP, 16, width), BF16),
+            pltpu.VMEM((2, N_EXP, 8, width), BF16),
+            pltpu.VMEM((2, N_EXP, 8, width), BF16),
             pltpu.VMEM((2, N_Y, ROWS, width), BF16),
             pltpu.VMEM((N_Y, ROWS, width), F32),
             pltpu.VMEM((2, hidden, width), BF16),
@@ -328,8 +289,8 @@
             pltpu.VMEM((2, 7, HALF, width), BF16),
             pltpu.VMEM((N_EXP, 8, width), BF16),
             pltpu.VMEM((N_EXP, 8, width), BF16),
-            dma((N_EXP,)), dma((N_EXP,)),
-            dma((2, 7)), dma((2, 7)),
+            dma((2, N_EXP)), dma((2, N_EXP)),
+            dma((2, 8)), dma((2, 8)),
             dma((2,)), dma((2,)),
             dma((2,)), dma((2,)),
             dma((2, 7)), dma((2, 7)),

time: 161 us -> 126 us (0.78)
  Pallas kernels: 156 us -> 121 us
    pallas_call x1, Pallas kernels: 156 us -> 121 us  [body(): pl.pallas_call(kernel, out_shape=(jax.ShapeDtypeStruct((tokens, width), B...]
where the time goes in v2:
time: 126 us
  Pallas kernels  121 us (96%)
  local copies, waits for them, and re-layouts  4.19 us (3%)
    pallas_call x1, Pallas kernels, body(): pl.pallas_call(kernel, out_shape=(jax.ShapeDtypeStruct((tokens, width), B...  121 us
    unnamed x5, local copies, waits for them, and re-layouts  4.19 us

profile of v2, /device:TPU:1, one launch (start us, length us, event | category | flops | bytes accessed | tf_op | source)
XLA Modules:
  0.0 126.1 jit_solution(499814507193166971)
XLA Ops:
  0.6 121.3 %moe_backward.1 = (bf16[128,640]{1,0:T(8,128)(2,1)}, bf16[320,640]{1,0:T(8,128)(2,1)}, bf16[320,640]{1,0:T(8,128)(2,1)}) custom-call(bf16[128,640]{1,0:T(8,128)(2,1)} %x_ref.1, bf16[128,640]{1,0:T(8,128)(2,1)} %g_ref.1, f32[2,128]{1,0:T(2,128)} %bitcast.16, s32[2,128]{1,0:T(2,128)} %bitcast.17, s32[2,128]{1,0:T(2,128)} %bitcast.18, s32[2,128]{1,0:T(2,128)} %bitcast.19, ...), custom_call_target="tpu_custom_call" | custom-call | tf_op jit(solution)/shard_map/moe_backward/pallas_call | solution.py:269
  121.9 1.6 %copy.14 = bf16[128,640]{1,0:T(8,128)(2,1)} copy(bf16[128,640]{1,0:T(8,128)(2,1)} %get-tuple-element.12) | data formatting | bytes 327680
  123.5 0.0 copy-start
  123.5 1.8 %copy.15 = bf16[1,640,320]{1,2,0:T(8,128)(2,1)} copy(bf16[1,640,320]{1,2,0:T(8,128)(2,1)} %bitcast.15) | data formatting | bytes 819200
  125.4 0.0 copy-done
  125.4 0.8 copy.16
Async XLA Ops:
  123.5 1.8 %copy-start = (bf16[320,640]{1,0:T(8,128)(2,1)S(1)}, bf16[320,640]{1,0:T(8,128)(2,1)}, u32[]{:S(2)}) copy-start(bf16[320,640]{1,0:T(8,128)(2,1)} %get-tuple-element.8) | copy-start | bytes 1228804

commit v3 on v2

--- a/solution.py
+++ b/solution.py
@@ -121,9 +121,17 @@
             return remote(rows.at[s, src, cut], rows.at[s, 1, cut], *sems)
         return remote(rows.at[s, src], rows.at[s, 2 * n + 2 + way], *sems)
 
+    mid = win_ref.shape[0] // 2
+    cuts = [pl.ds(0, mid), pl.ds(mid, mid)]
     weights = [
-        remote(win_ref, wp.at[0], w_s.at[0], w_r.at[0], mate),
-        remote(wout_ref, wp.at[1], w_s.at[1], w_r.at[1], mate),
+        remote(ref.at[cut], wp.at[i, cut], w_s.at[h, i], w_r.at[h, i], mate)
+        for h, cut in enumerate(cuts)
+        for i, ref in enumerate((win_ref, wout_ref))
+    ]
+    deltas = [
+        remote(dw_out.at[i, cut], dw_in.at[i, cut], dw_s.at[h, i], dw_r.at[h, i], mate)
+        for h, cut in enumerate(cuts)
+        for i in range(2)
     ]
     for s in range(2):
         each_peer(lambda k: a2a_from(s, k).wait_recv())
@@ -134,56 +142,60 @@
     for copy in weights:
         copy.start()
 
-    def core(b, half, wi, wo, gp_at):
+    def core(b, half, wi, wo, cut):
         ri = rows[0, pl.ds(2 * b, 2)].reshape(2 * ROWS, -1)
         rc = rows[1, pl.ds(2 * b, 2)].reshape(2 * ROWS, -1)
-        pre = dot(wi[...], ri, NT)
-        bp = dot(wo[...], rc, NT)
+        pre = dot(wi[cut], ri, NT)
+        bp = dot(wo[cut], rc, NT)
         sq = pre * pre
         h = jnp.tanh(ROOT_COEF * (pre + CUBE_COEF * sq * pre))
         up = 0.5 * (1.0 + h)
         slope = up + 0.5 * pre * (1.0 - h * h) * ROOT_COEF * (1.0 + 3.0 * CUBE_COEF * sq)
         g = (slope * bp).astype(BF16)
-        gp_at[...] = g
-        dw[half, 0] += dot(g, ri, NN)
-        dw[half, 1] += dot((pre * up).astype(BF16), rc, NN)
-
-    def project(b, wi, gp_at, first):
-        p = dot(gp_at[...], wi[...], TN).reshape(2, ROWS, -1)
-        if first:
+        gp[half, b, cut] = g
+        dw[half, 0, cut] += dot(g, ri, NN)
+        dw[half, 1, cut] += dot((pre * up).astype(BF16), rc, NN)
+
+    def project(b, half, wi):
+        p = dot(gp[half, b], wi[...], TN).reshape(2, ROWS, -1)
+        if half == 0:
             part[pl.ds(2 * b, 2)] = p
         else:
             part[pl.ds(2 * b, 2)] += p
 
+    whole = pl.ds(0, 2 * mid)
     for n in range(1, 4):
         for i in (2 * n - 2, 2 * n - 1):
             for way in range(2):
                 gather(way, i).wait_recv()
                 gather(way, i + 2).start()
-        core(n, 0, win_ref, wout_ref, gp.at[0])
-        project(n, win_ref, gp.at[0], True)
-
-    for copy in weights:
-        copy.wait_recv()
-
-    def mate_step(n, c):
-        core(n, 1, wp.at[0], wp.at[1], gp.at[1])
-        project(n, wp.at[0], gp.at[1], False)
-        return c
-
-    lax.fori_loop(1, 4, mate_step, 0)
-
-    for i in (6, 7):
-        for way in range(2):
-            gather(way, i).wait_recv()
-    core(0, 1, wp.at[0], wp.at[1], gp.at[1])
-    dw_out[...] = dw[1].astype(BF16)
-    deltas = [remote(dw_out.at[i], dw_in.at[i], dw_s.at[i], dw_r.at[i], mate) for i in range(2)]
-    for copy in deltas:
-        copy.start()
-    core(0, 0, win_ref, wout_ref, gp.at[0])
-    project(0, win_ref, gp.at[0], True)
-    project(0, wp.at[0], gp.at[1], False)
+        core(n, 0, win_ref, wout_ref, whole)
+        project(n, 0, win_ref)
+
+    for h, cut in enumerate(cuts):
+        for copy in weights[2 * h : 2 * h + 2]:
+            copy.wait_recv()
+
+        def mate_step(b, c):
+            core(b, 1, wp.at[0], wp.at[1], cut)
+            return c
+
+        if h == 0:
+            lax.fori_loop(1, 4, mate_step, 0)
+            for i in (6, 7):
+                for way in range(2):
+                    gather(way, i).wait_recv()
+            mate_step(0, 0)
+        else:
+            lax.fori_loop(0, 4, mate_step, 0)
+        for i in range(2):
+            dw_out[i, cut] = dw[1, i, cut].astype(BF16)
+            deltas[2 * h + i].start()
+        if h == 0:
+            core(0, 0, win_ref, wout_ref, whole)
+            project(0, 0, win_ref)
+    for b in (0, 3, 2, 1):
+        project(b, 1, wp.at[0])
 
     def ring(way, i):
         return remote(
@@ -254,11 +266,17 @@
     out_ref[...] = dot(pick, returned, NN).astype(BF16)
     each_peer(lambda k: back(k).wait_send())
 
-    for i, ref in ((0, owin_ref), (1, owout_ref)):
-        deltas[i].wait_recv()
-        ref[...] = (dw[0, i] + dw_in[i].astype(F32)).astype(BF16)
+    for h, cut in enumerate(cuts):
+        for i, ref in enumerate((owin_ref, owout_ref)):
+            deltas[2 * h + i].wait_recv()
+            ref[cut] = (dw[0, i, cut] + dw_in[i, cut].astype(F32)).astype(BF16)
     for copy in deltas:
         copy.wait_send()
+
+
+def hand_over(*refs):
+    for src, dst in zip(refs[:3], refs[3:]):
+        dst[...] = src[...]
 
 
 def body(x, g, gate, eid, slot, keep, weight_in, weight_out):
@@ -266,13 +284,14 @@
     hidden = weight_in.shape[2]
     dma = pltpu.SemaphoreType.DMA
     vmem = pl.BlockSpec(memory_space=pltpu.VMEM)
-    out, dwin, dwout = pl.pallas_call(
+    shapes = (
+        jax.ShapeDtypeStruct((tokens, width), BF16),
+        jax.ShapeDtypeStruct((hidden, width), BF16),
+        jax.ShapeDtypeStruct((hidden, width), BF16),
+    )
+    results = pl.pallas_call(
         kernel,
-        out_shape=(
-            jax.ShapeDtypeStruct((tokens, width), BF16),
-            jax.ShapeDtypeStruct((hidden, width), BF16),
-            jax.ShapeDtypeStruct((hidden, width), BF16),
-        ),
+        out_shape=shapes,
         in_specs=[vmem] * 8,
         out_specs=(vmem, vmem, vmem),
         scratch_shapes=[
@@ -284,15 +303,15 @@
             pltpu.VMEM((2, 2, hidden, width), F32),
             pltpu.VMEM((2, hidden, width), BF16),
             pltpu.VMEM((2, hidden, width), BF16),
-            pltpu.VMEM((2, hidden, 2 * ROWS), BF16),
+            pltpu.VMEM((2, N_Y // 2, hidden, 2 * ROWS), BF16),
             pltpu.VMEM((2, 7, HALF, width), BF16),
             pltpu.VMEM((2, 7, HALF, width), BF16),
             pltpu.VMEM((N_EXP, 8, width), BF16),
             pltpu.VMEM((N_EXP, 8, width), BF16),
             dma((2, N_EXP)), dma((2, N_EXP)),
             dma((2, 8)), dma((2, 8)),
-            dma((2,)), dma((2,)),
-            dma((2,)), dma((2,)),
+            dma((2, 2)), dma((2, 2)),
+            dma((2, 2)), dma((2, 2)),
             dma((2, 7)), dma((2, 7)),
             dma((N_EXP,)), dma((N_EXP,)),
         ],
@@ -304,6 +323,9 @@
         x, g, gate.T, eid.T, slot.T, keep.T,
         jnp.swapaxes(weight_in[0], 0, 1), weight_out[0],
     )
+    out, dwin, dwout = pl.pallas_call(
+        hand_over, out_shape=shapes, in_specs=[vmem] * 3, out_specs=(vmem,) * 3, name="hand_over"
+    )(*results)
     return out, jnp.swapaxes(dwin, 0, 1)[None], dwout[None]
 
 

time: 126 us -> 120 us (0.952)
  local copies, waits for them, and re-layouts: 4.19 us -> 0 us
  Pallas kernels: 121 us -> 119 us
    unnamed x5 -> x0, local copies, waits for them, and re-layouts: 4.19 us -> none
    pallas_call x1 -> x2, Pallas kernels: 121 us -> 119 us  [the longest x1 117 us: body(): pl.pallas_call(kernel, out_shape=shapes, in_specs=[vmem] * 8, out_specs=(...]
where the time goes in v3:
time: 120 us
  Pallas kernels  119 us (99%)
    pallas_call x1, Pallas kernels, body(): pl.pallas_call(kernel, out_shape=shapes, in_specs=[vmem] * 8, out_specs=(...  117 us

profile of v3, /device:TPU:1, one launch (start us, length us, event | category | flops | bytes accessed | tf_op | source)
XLA Modules:
  0.0 120.0 jit_solution(2992863190820725896)
XLA Ops:
  0.6 117.2 %moe_backward.1 = (bf16[128,640]{1,0:T(8,128)(2,1)}, bf16[320,640]{1,0:T(8,128)(2,1)}, bf16[320,640]{1,0:T(8,128)(2,1)}) custom-call(bf16[128,640]{1,0:T(8,128)(2,1)} %x_ref.1, bf16[128,640]{1,0:T(8,128)(2,1)} %g_ref.1, f32[2,128]{1,0:T(2,128)} %bitcast.14, s32[2,128]{1,0:T(2,128)} %bitcast.15, s32[2,128]{1,0:T(2,128)} %bitcast.16, s32[2,128]{1,0:T(2,128)} %bitcast.17, ...), custom_call_target="tpu_custom_call" | custom-call | tf_op jit(solution)/shard_map/moe_backward/pallas_call | solution.py:292
  117.8 2.2 %hand_over.1 = (bf16[128,640]{1,0:T(8,128)(2,1)}, bf16[320,640]{1,0:T(8,128)(2,1)}, bf16[320,640]{1,0:T(8,128)(2,1)}) custom-call(bf16[128,640]{1,0:T(8,128)(2,1)} %get-tuple-element.9.refs_0_, bf16[320,640]{1,0:T(8,128)(2,1)} %get-tuple-element.10.refs_1_, bf16[320,640]{1,0:T(8,128)(2,1)} %get-tuple-element.11.refs_2_), custom_call_target="tpu_custom_call" | custom-call | tf_op jit(solution)/shard_map/hand_over/pallas_call | solution.py:326

commit v4 on v3

--- a/solution.py
+++ b/solution.py
@@ -13,6 +13,9 @@
 CAP = 6
 ROWS = N_EXP * CAP
 HALF = ROWS // 2
+LANES = 128
+BLOCK = 32
+GROUP = 8
 BF16 = jnp.bfloat16
 F32 = jnp.float32
 
@@ -67,22 +70,53 @@
     for device in (right, left, mate):
         pl.semaphore_signal(barrier, 1, device_id=device, device_id_type=MESH)
 
-    tokens = x_ref.shape[0]
-    blk = N_EXP * 8
-    eid = eid_ref[...].astype(F32)
-    slot = slot_ref[...].astype(F32)
-    target = jnp.where(keep_ref[...] > 0, eid * 8.0 + slot, -100.0)
-    row_id = iota((blk, tokens), 0).astype(F32)
+    tokens, width = x_ref.shape
+    tiles = width // LANES
+    few = GROUP * CAP
+
+    def packed_at(shape, dim):
+        r = iota(shape, dim)
+        inside = jnp.bitwise_and(r, BLOCK - 1)
+        tile = lax.shift_right_logical(inside * 43, 8)
+        at = tile * few + lax.shift_right_logical(r, 5) * CAP + inside - tile * CAP
+        return jnp.where(inside < tiles * CAP, at, -1)
+
+    wide = (GROUP * BLOCK, tiles * few)
+    tall = (tiles * few, GROUP * BLOCK)
+    spread = jnp.where(iota(wide, 1) == packed_at(wide, 0), 1.0, 0.0).astype(BF16)
+    close = jnp.where(iota(tall, 0) == packed_at(tall, 1), 1.0, 0.0).astype(BF16)
+
+    def pack(value, dst):
+        for n in range(N_EXP // GROUP):
+            some = value[n * few : (n + 1) * few]
+            stack = jnp.concatenate(
+                [some[:, t * LANES : (t + 1) * LANES] for t in range(tiles)], axis=0
+            )
+            out = dot(spread, stack, NN).astype(BF16)
+            dst[pl.ds(n * GROUP, GROUP)] = out.reshape(GROUP, BLOCK, LANES)
+
+    def unpack(src, n):
+        out = dot(close, src[pl.ds(n * GROUP, GROUP)].reshape(GROUP * BLOCK, LANES), NN)
+        out = out.astype(BF16)
+        return jnp.concatenate([out[t * few : (t + 1) * few] for t in range(tiles)], axis=1)
+
+    target = jnp.where(
+        keep_ref[...] > 0, eid_ref[...].astype(F32) * float(CAP) + slot_ref[...].astype(F32), -100.0
+    )
+    row_id = iota((ROWS, tokens), 0).astype(F32)
     hots = [
-        jnp.where(row_id == jnp.broadcast_to(target[k : k + 1], (blk, tokens)), 1.0, 0.0)
+        jnp.where(row_id == jnp.broadcast_to(target[k : k + 1], (ROWS, tokens)), 1.0, 0.0)
         for k in range(2)
     ]
-    send[0] = dot((hots[0] + hots[1]).astype(BF16), x_ref[...], NN).astype(BF16).reshape(send.shape[1:])
+    pack(dot((hots[0] + hots[1]).astype(BF16), x_ref[...], NN).astype(BF16), send.at[0])
     grad = g_ref[...].astype(F32)
     scaled = [(column(gate_ref[k : k + 1]) * grad).astype(BF16) for k in range(2)]
-    send[1] = dot(
-        jnp.concatenate(hots, axis=1).astype(BF16), jnp.concatenate(scaled, axis=0), NN
-    ).astype(BF16).reshape(send.shape[1:])
+    pack(
+        dot(
+            jnp.concatenate(hots, axis=1).astype(BF16), jnp.concatenate(scaled, axis=0), NN
+        ).astype(BF16),
+        send.at[1],
+    )
     for s in range(2):
         recv[s, pl.ds(e, 1)] = send[s, pl.ds(e, 1)]
     dw[...] = jnp.zeros_like(dw)
@@ -106,11 +140,6 @@
 
     for s in range(2):
         each_peer(lambda k: a2a(s, k).start())
-
-    q = iota((ROWS, blk), 1)
-    lane = jnp.bitwise_and(q, 7)
-    want = jnp.where(lane < CAP, lax.shift_right_logical(q, 3) * CAP + lane, -1)
-    close = jnp.where(iota((ROWS, blk), 0) == want, 1.0, 0.0).astype(BF16)
 
     def gather(way, i):
         s, n = i % 2, i // 2
@@ -135,8 +164,8 @@
     ]
     for s in range(2):
         each_peer(lambda k: a2a_from(s, k).wait_recv())
-        arrived = recv[s].astype(F32).reshape(blk, -1).astype(BF16)
-        rows[s, 0] = dot(close, arrived, NN).astype(BF16)
+        for n in range(N_EXP // GROUP):
+            rows[s, 0, pl.ds(n * few, few)] = unpack(recv.at[s], n)
         for way in range(2):
             gather(way, s).start()
     for copy in weights:
@@ -217,14 +246,8 @@
             rs_out[way, i] = value.astype(BF16)
             ring(way, i).start()
 
-    spread_q = iota((blk, ROWS), 0)
-    spread_lane = jnp.bitwise_and(spread_q, 7)
-    spread_want = jnp.where(
-        spread_lane < CAP, lax.shift_right_logical(spread_q, 3) * CAP + spread_lane, -1
-    )
-    spread = jnp.where(iota((blk, ROWS), 1) == spread_want, 1.0, 0.0).astype(BF16)
-    column_id = iota((tokens, blk), 1).astype(F32)
-    pick = jnp.zeros((tokens, blk), F32)
+    column_id = iota((tokens, ROWS), 1).astype(F32)
+    pick = jnp.zeros((tokens, ROWS), F32)
     for k in range(2):
         pick = pick + jnp.where(column_id == column(target[k : k + 1]), 1.0, 0.0)
     pick = pick.astype(BF16)
@@ -240,7 +263,7 @@
             value = value + rs_in[way, i].astype(F32)
         sums.append(value.astype(BF16))
     total = jnp.concatenate(sums, axis=0)
-    back_out[...] = dot(spread, total, NN).reshape(back_out.shape).astype(BF16)
+    pack(total, back_out)
     back_in[pl.ds(e, 1)] = back_out[pl.ds(e, 1)]
 
     def back(k):
@@ -262,7 +285,7 @@
         for i in range(7):
             ring(way, i).wait_send()
     each_peer(lambda k: back_from(k).wait_recv())
-    returned = back_in[...].astype(F32).reshape(blk, -1).astype(BF16)
+    returned = jnp.concatenate([unpack(back_in, n) for n in range(N_EXP // GROUP)], axis=0)
     out_ref[...] = dot(pick, returned, NN).astype(BF16)
     each_peer(lambda k: back(k).wait_send())
 
@@ -295,8 +318,8 @@
         in_specs=[vmem] * 8,
         out_specs=(vmem, vmem, vmem),
         scratch_shapes=[
-            pltpu.VMEM((2, N_EXP, 8, width), BF16),
-            pltpu.VMEM((2, N_EXP, 8, width), BF16),
+            pltpu.VMEM((2, N_EXP, BLOCK, LANES), BF16),
+            pltpu.VMEM((2, N_EXP, BLOCK, LANES), BF16),
             pltpu.VMEM((2, N_Y, ROWS, width), BF16),
             pltpu.VMEM((N_Y, ROWS, width), F32),
             pltpu.VMEM((2, hidden, width), BF16),
@@ -306,8 +329,8 @@
             pltpu.VMEM((2, N_Y // 2, hidden, 2 * ROWS), BF16),
             pltpu.VMEM((2, 7, HALF, width), BF16),
             pltpu.VMEM((2, 7, HALF, width), BF16),
-            pltpu.VMEM((N_EXP, 8, width), BF16),
-            pltpu.VMEM((N_EXP, 8, width), BF16),
+            pltpu.VMEM((N_EXP, BLOCK, LANES), BF16),
+            pltpu.VMEM((N_EXP, BLOCK, LANES), BF16),
             dma((2, N_EXP)), dma((2, N_EXP)),
             dma((2, 8)), dma((2, 8)),
             dma((2, 2)), dma((2, 2)),

time: 120 us -> 117 us (0.975)
  Pallas kernels: 119 us -> 116 us
    pallas_call x1, Pallas kernels: 117 us -> 114 us  [body(): pl.pallas_call(kernel, out_shape=shapes, in_specs=[vmem] * 8, out_specs=(...]
where the time goes in v4:
time: 117 us
  Pallas kernels  116 us (99%)
    pallas_call x1, Pallas kernels, body(): pl.pallas_call(kernel, out_shape=shapes, in_specs=[vmem] * 8, out_specs=(...  114 us

profile of v4, /device:TPU:1, one launch (start us, length us, event | category | flops | bytes accessed | tf_op | source)
XLA Modules:
  0.0 117.1 jit_solution(958944875276519196)
XLA Ops:
  0.6 114.3 %moe_backward.1 = (bf16[128,640]{1,0:T(8,128)(2,1)}, bf16[320,640]{1,0:T(8,128)(2,1)}, bf16[320,640]{1,0:T(8,128)(2,1)}) custom-call(bf16[128,640]{1,0:T(8,128)(2,1)} %x_ref.1, bf16[128,640]{1,0:T(8,128)(2,1)} %g_ref.1, f32[2,128]{1,0:T(2,128)} %bitcast.14, s32[2,128]{1,0:T(2,128)} %bitcast.15, s32[2,128]{1,0:T(2,128)} %bitcast.16, s32[2,128]{1,0:T(2,128)} %bitcast.17, ...), custom_call_target="tpu_custom_call" | custom-call | tf_op jit(solution)/shard_map/moe_backward/pallas_call | solution.py:315
  114.9 2.2 %hand_over.1 = (bf16[128,640]{1,0:T(8,128)(2,1)}, bf16[320,640]{1,0:T(8,128)(2,1)}, bf16[320,640]{1,0:T(8,128)(2,1)}) custom-call(bf16[128,640]{1,0:T(8,128)(2,1)} %get-tuple-element.9.refs_0_, bf16[320,640]{1,0:T(8,128)(2,1)} %get-tuple-element.10.refs_1_, bf16[320,640]{1,0:T(8,128)(2,1)} %get-tuple-element.11.refs_2_), custom_call_target="tpu_custom_call" | custom-call | tf_op jit(solution)/shard_map/hand_over/pallas_call | solution.py:349

commit v5 on v4

--- a/solution.py
+++ b/solution.py
@@ -41,8 +41,9 @@
 
 def kernel(
     x_ref, g_ref, gate_ref, eid_ref, slot_ref, keep_ref, win_ref, wout_ref,
-    out_ref, owin_ref, owout_ref,
+    out_hbm, owin_hbm, owout_hbm,
     send, recv, rows, part, wp, dw, dw_out, dw_in, gp, rs_out, rs_in, back_out, back_in,
+    out_ref, ow_ref, done,
     a2a_s, a2a_r, ag_s, ag_r, w_s, w_r, dw_s, dw_r, rs_s, rs_r, back_s, back_r,
 ):
     d = lax.axis_index("dp")
@@ -287,14 +288,22 @@
     each_peer(lambda k: back_from(k).wait_recv())
     returned = jnp.concatenate([unpack(back_in, n) for n in range(N_EXP // GROUP)], axis=0)
     out_ref[...] = dot(pick, returned, NN).astype(BF16)
+    results = [pltpu.make_async_copy(out_ref, out_hbm, done.at[0])]
+    results[0].start()
     each_peer(lambda k: back(k).wait_send())
 
     for h, cut in enumerate(cuts):
-        for i, ref in enumerate((owin_ref, owout_ref)):
+        for i, ref in enumerate((owin_hbm, owout_hbm)):
             deltas[2 * h + i].wait_recv()
-            ref[cut] = (dw[0, i, cut] + dw_in[i, cut].astype(F32)).astype(BF16)
+            ow_ref[i, cut] = (dw[0, i, cut] + dw_in[i, cut].astype(F32)).astype(BF16)
+            results.append(
+                pltpu.make_async_copy(ow_ref.at[i, cut], ref.at[cut], done.at[1 + 2 * h + i])
+            )
+            results[-1].start()
     for copy in deltas:
         copy.wait_send()
+    for copy in results:
+        copy.wait()
 
 
 def hand_over(*refs):
@@ -316,7 +325,7 @@
         kernel,
         out_shape=shapes,
         in_specs=[vmem] * 8,
-        out_specs=(vmem, vmem, vmem),
+        out_specs=(pl.BlockSpec(memory_space=pl.ANY),) * 3,
         scratch_shapes=[
             pltpu.VMEM((2, N_EXP, BLOCK, LANES), BF16),
             pltpu.VMEM((2, N_EXP, BLOCK, LANES), BF16),
@@ -331,6 +340,9 @@
             pltpu.VMEM((2, 7, HALF, width), BF16),
             pltpu.VMEM((N_EXP, BLOCK, LANES), BF16),
             pltpu.VMEM((N_EXP, BLOCK, LANES), BF16),
+            pltpu.VMEM((tokens, width), BF16),
+            pltpu.VMEM((2, hidden, width), BF16),
+            dma((5,)),
             dma((2, N_EXP)), dma((2, N_EXP)),
             dma((2, 8)), dma((2, 8)),
             dma((2, 2)), dma((2, 2)),
@@ -339,16 +351,14 @@
             dma((N_EXP,)), dma((N_EXP,)),
         ],
         compiler_params=pltpu.CompilerParams(
-            collective_id=0, has_side_effects=True, vmem_limit_bytes=56 * 1024 * 1024
+            collective_id=0, has_side_effects=True, vmem_limit_bytes=36 * 1024 * 1024
         ),
         name="moe_backward",
     )(
         x, g, gate.T, eid.T, slot.T, keep.T,
         jnp.swapaxes(weight_in[0], 0, 1), weight_out[0],
     )
-    out, dwin, dwout = pl.pallas_call(
-        hand_over, out_shape=shapes, in_specs=[vmem] * 3, out_specs=(vmem,) * 3, name="hand_over"
-    )(*results)
+    out, dwin, dwout = results
     return out, jnp.swapaxes(dwin, 0, 1)[None], dwout[None]
 
 

time: 117 us -> 121 us (1.034)
  local copies, waits for them, and re-layouts: 0 us -> 6.7 us
  Pallas kernels: 116 us -> 114 us
    unnamed x0 -> x19, local copies, waits for them, and re-layouts: none -> 6.7 us
    pallas_call x1 -> x0, Pallas kernels: 2.18 us -> none  [body(): pl.pallas_call(hand_over, out_shape=shapes, in_specs=[vmem] * 3, out_spec...]
where the time goes in v5:
time: 121 us
  Pallas kernels  114 us (94%)
  local copies, waits for them, and re-layouts  6.7 us (6%)
    pallas_call x1, Pallas kernels, body(): pl.pallas_call(kernel, out_shape=shapes, in_specs=[vmem] * 8, out_specs=(...  114 us
    unnamed x19, local copies, waits for them, and re-layouts  6.7 us

profile of v5, /device:TPU:1, one launch (start us, length us, event | category | flops | bytes accessed | tf_op | source)
XLA Modules:
  0.0 121.1 jit_solution(1194666549231545352)
XLA Ops:
  0.6 0.0 copy-start.7
  0.6 0.0 copy-start.5
  0.7 0.0 copy-start.6
  0.7 0.0 copy-start.4
  0.7 0.6 copy-done.7
  1.3 0.0 copy-done.5
  1.3 0.0 copy-done.6
  1.3 0.0 copy-done.4
  1.4 0.0 copy-start
  1.4 1.0 copy-done
  2.4 0.0 copy-start.1
  2.4 1.0 copy-done.1
  3.4 0.0 copy-start.2
  3.4 0.9 copy-done.2
  4.3 0.0 copy-start.3
  4.3 0.9 copy-done.3
  5.2 113.8 %moe_backward.1 = (bf16[128,640]{1,0:T(8,128)(2,1)S(1)}, bf16[320,640]{1,0:T(8,128)(2,1)S(1)}, bf16[320,640]{1,0:T(8,128)(2,1)S(1)}) custom-call(bf16[128,640]{1,0:T(8,128)(2,1)S(1)} %copy-done.2, bf16[128,640]{1,0:T(8,128)(2,1)S(1)} %copy-done.3, f32[2,128]{1,0:T(2,128)S(1)} %bitcast.16, s32[2,128]{1,0:T(2,128)S(1)} %bitcast.17, s32[2,128]{1,0:T(2,128)S(1)} %bitcast.18, ...), custom_call_target="tpu_custom_call" | custom-call | tf_op jit(solution)/shard_map/moe_backward/pallas_call | solution.py:324
  119.0 0.7 copy.14
  119.6 0.8 copy.15
  120.4 0.8 copy.16
Async XLA Ops:
  0.6 0.7 copy-start.7
  0.6 0.7 copy-start.5
  0.7 0.7 copy-start.6
  0.7 0.7 copy-start.4
  1.4 1.0 copy-start
  2.4 1.0 copy-start.1
  3.4 0.9 copy-start.2
  4.3 0.9 copy-start.3

commit v6 on v5

--- a/solution.py
+++ b/solution.py
@@ -40,8 +40,9 @@
 
 
 def kernel(
-    x_ref, g_ref, gate_ref, eid_ref, slot_ref, keep_ref, win_ref, wout_ref,
+    x_hbm, g_hbm, gate_hbm, eid_hbm, slot_hbm, keep_hbm, win_hbm, wout_hbm,
     out_hbm, owin_hbm, owout_hbm,
+    x_ref, g_ref, gate_ref, eid_ref, slot_ref, keep_ref, win_ref, wout_ref, load,
     send, recv, rows, part, wp, dw, dw_out, dw_in, gp, rs_out, rs_in, back_out, back_in,
     out_ref, ow_ref, done,
     a2a_s, a2a_r, ag_s, ag_r, w_s, w_r, dw_s, dw_r, rs_s, rs_r, back_s, back_r,
@@ -71,6 +72,15 @@
     for device in (right, left, mate):
         pl.semaphore_signal(barrier, 1, device_id=device, device_id_type=MESH)
 
+    sources = (x_hbm, g_hbm, gate_hbm, eid_hbm, slot_hbm, keep_hbm, win_hbm, wout_hbm)
+    places = (x_ref, g_ref, gate_ref, eid_ref, slot_ref, keep_ref, win_ref, wout_ref)
+    loads = [
+        pltpu.make_async_copy(source, place, load.at[i])
+        for i, (source, place) in enumerate(zip(sources, places))
+    ]
+    for copy in loads:
+        copy.start()
+
     tokens, width = x_ref.shape
     tiles = width // LANES
     few = GROUP * CAP
@@ -101,6 +111,8 @@
         out = out.astype(BF16)
         return jnp.concatenate([out[t * few : (t + 1) * few] for t in range(tiles)], axis=1)
 
+    for copy in loads:
+        copy.wait()
     target = jnp.where(
         keep_ref[...] > 0, eid_ref[...].astype(F32) * float(CAP) + slot_ref[...].astype(F32), -100.0
     )
@@ -324,9 +336,18 @@
     results = pl.pallas_call(
         kernel,
         out_shape=shapes,
-        in_specs=[vmem] * 8,
+        in_specs=[pl.BlockSpec(memory_space=pl.ANY)] * 8,
         out_specs=(pl.BlockSpec(memory_space=pl.ANY),) * 3,
         scratch_shapes=[
+            pltpu.VMEM((tokens, width), BF16),
+            pltpu.VMEM((tokens, width), BF16),
+            pltpu.VMEM((2, tokens), F32),
+            pltpu.VMEM((2, tokens), jnp.int32),
+            pltpu.VMEM((2, tokens), jnp.int32),
+            pltpu.VMEM((2, tokens), jnp.int32),
+            pltpu.VMEM((hidden, width), BF16),
+            pltpu.VMEM((hidden, width), BF16),
+            dma((8,)),
             pltpu.VMEM((2, N_EXP, BLOCK, LANES), BF16),
             pltpu.VMEM((2, N_EXP, BLOCK, LANES), BF16),
             pltpu.VMEM((2, N_Y, ROWS, width), BF16),
@@ -351,14 +372,16 @@
             dma((N_EXP,)), dma((N_EXP,)),
         ],
         compiler_params=pltpu.CompilerParams(
-            collective_id=0, has_side_effects=True, vmem_limit_bytes=36 * 1024 * 1024
+            collective_id=0, has_side_effects=True, vmem_limit_bytes=56 * 1024 * 1024
         ),
         name="moe_backward",
     )(
         x, g, gate.T, eid.T, slot.T, keep.T,
         jnp.swapaxes(weight_in[0], 0, 1), weight_out[0],
     )
-    out, dwin, dwout = results
+    out, dwin, dwout = pl.pallas_call(
+        hand_over, out_shape=shapes, in_specs=[vmem] * 3, out_specs=(vmem,) * 3, name="hand_over"
+    )(*results)
     return out, jnp.swapaxes(dwin, 0, 1)[None], dwout[None]
 
 

time: 121 us -> 116 us (0.959)
  local copies, waits for them, and re-layouts: 6.7 us -> 0 us
  Pallas kernels: 114 us -> 116 us
    unnamed x19 -> x0, local copies, waits for them, and re-layouts: 6.7 us -> none
    pallas_call x1 -> x2, Pallas kernels: 114 us -> 116 us  [the longest x1 113 us: body(): pl.pallas_call(kernel, out_shape=shapes, in_specs=[pl.BlockSpec(memory_sp...]
where the time goes in v6:
time: 116 us
  Pallas kernels  116 us (100%)
    pallas_call x1, Pallas kernels, body(): pl.pallas_call(kernel, out_shape=shapes, in_specs=[pl.BlockSpec(memory_sp...  113 us

profile of v6, /device:TPU:1, one launch (start us, length us, event | category | flops | bytes accessed | tf_op | source)
XLA Modules:
  0.0 116.2 jit_solution(13498978790436184992)
XLA Ops:
  0.6 113.4 %moe_backward.1 = (bf16[128,640]{1,0:T(8,128)(2,1)}, bf16[320,640]{1,0:T(8,128)(2,1)}, bf16[320,640]{1,0:T(8,128)(2,1)}) custom-call(bf16[128,640]{1,0:T(8,128)(2,1)} %x_hbm.1, bf16[128,640]{1,0:T(8,128)(2,1)} %g_hbm.1, f32[2,128]{1,0:T(2,128)} %bitcast.14, s32[2,128]{1,0:T(2,128)} %bitcast.15, s32[2,128]{1,0:T(2,128)} %bitcast.16, s32[2,128]{1,0:T(2,128)} %bitcast.17, ...), custom_call_target="tpu_custom_call" | custom-call | tf_op jit(solution)/shard_map/moe_backward/pallas_call | solution.py:336
  114.0 2.2 %hand_over.1 = (bf16[128,640]{1,0:T(8,128)(2,1)}, bf16[320,640]{1,0:T(8,128)(2,1)}, bf16[320,640]{1,0:T(8,128)(2,1)}) custom-call(bf16[128,640]{1,0:T(8,128)(2,1)} %get-tuple-element.9.refs_0_, bf16[320,640]{1,0:T(8,128)(2,1)} %get-tuple-element.10.refs_1_, bf16[320,640]{1,0:T(8,128)(2,1)} %get-tuple-element.11.refs_2_), custom_call_target="tpu_custom_call" | custom-call | tf_op jit(solution)/shard_map/hand_over/pallas_call | solution.py:382
